TPU v7x, 32 devices: a whole 2x2x4 slice. The times are simulated.
32 devices in a mesh: slab: 2 (over y), bx: 8 (over z, x), by: 2 (over core).
Axes of the slice: x: 2, y: 2, z: 4, core: 2. Of those that a mesh axis runs over, the one named last changes fastest.
Arguments:
- phi: float32 [64, 128, 2048], P('slab', 'bx', 'by'), parts along dimension 0, may hold values from -6 to 6
- first_measurement: float32 [128, 2048], P('slab', 'by'), parts along dimension 0, may hold values from 0.5 to 3.5
- second_measurement: float32 [128, 128], P('slab', 'bx'), parts along dimension 0, may hold values from 0.5 to 3.5
- first_view_mask: int32 [128, 2048], P('slab', 'by'), parts along dimension 0, may hold values 0 or 1
- second_view_mask: int32 [128, 128], P('slab', 'bx'), parts along dimension 0, may hold values 0 or 1
- plane_detector_rows: int32 [32], replicated, may hold values from 0 to 63, as said below
Outputs:
- gradient: float32 [64, 128, 2048], P('slab', 'bx', 'by'), parts along dimension 0
There are 2 independent parts, one for each index of `slab`. A program takes and returns all parts, laid end to end along the dimension named above; an argument that names none is the same for every part. Nothing has to cross between parts.
Inputs may be any that keep to these rules, and one draw needn't show every extreme that they name: `plane_detector_rows`: plane z reads detector row 2 z or 2 z + 1; plane 0 reads row 0 and the last plane reads row 63.
All inputs are finite; a program needn't handle non-finite values. No bound on the sum of `first_view_mask` or of `second_view_mask` on one device may be relied on, other than what follows from the above.
Results may differ from a plain program's by a relative error of at most 0.00002.
Values sent between devices are 32-bit elements; how exact they have to be, the bound alone decides.
A program may use at most 64 MiB of HBM per device.

v0:
```python
import jax
import jax.numpy as jnp
from jax import lax
from jax.sharding import PartitionSpec as P

LAMBDA = 0.5
BETA2 = 1.0


def extended(cells, sides, width):
    for axis, dim in sides:
        count = lax.axis_size(axis)
        ends = count - 1
        head = lax.slice_in_dim(cells, 0, width, axis=dim)
        tail = lax.slice_in_dim(cells, cells.shape[dim] - width, cells.shape[dim], axis=dim)
        cells = jnp.concatenate(
            [
                lax.ppermute(tail, axis, [(i, (i + 1) % count) for i in range(ends)]),
                cells,
                lax.ppermute(head, axis, [((i + 1) % count, i) for i in range(ends)]),
            ],
            axis=dim,
        )
    return cells


def curvature_of(padded):
    core = padded[:-1, :-1, :-1]
    grad_z = padded[1:, :-1, :-1] - core
    grad_x = padded[:-1, 1:, :-1] - core
    grad_y = padded[:-1, :-1, 1:] - core
    magnitude = jnp.sqrt(grad_z * grad_z + grad_x * grad_x + grad_y * grad_y + BETA2)
    flux_z = grad_z / magnitude
    flux_x = grad_x / magnitude
    flux_y = grad_y / magnitude
    div_z = flux_z[1:, 1:, 1:] - flux_z[:-1, 1:, 1:]
    div_x = flux_x[1:, 1:, 1:] - flux_x[1:, :-1, 1:]
    div_y = flux_y[1:, 1:, 1:] - flux_y[1:, 1:, :-1]
    return div_z + div_x + div_y


def per_device(
    phi,
    first_measurement,
    second_measurement,
    first_view_mask,
    second_view_mask,
    plane_detector_rows,
):
    planes, cells_x, cells_y = phi.shape
    total_x = cells_x * lax.axis_size("bx")
    total_y = cells_y * lax.axis_size("by")
    tanh_phi = jnp.tanh(phi)
    heav = 0.5 * (1.0 + tanh_phi)
    slope = 0.5 * (1.0 - tanh_phi * tanh_phi)
    part_a = jnp.sum(heav, axis=1)
    part_b = jnp.sum(heav, axis=2)
    first_measured_rows = jnp.take(first_measurement, plane_detector_rows, axis=0)
    first_mask_rows = jnp.take(first_view_mask, plane_detector_rows, axis=0).astype(jnp.float32)
    second_measured_rows = jnp.take(second_measurement, plane_detector_rows, axis=0)
    second_mask_rows = jnp.take(second_view_mask, plane_detector_rows, axis=0).astype(jnp.float32)
    second_projection = lax.psum(part_b, "by") * (4.0 / total_y)
    second_residual = second_mask_rows * (second_projection - second_measured_rows)
    first_projection = lax.psum(part_a, "bx") * (4.0 / total_x)
    first_residual = first_mask_rows * (first_projection - first_measured_rows)
    padded = extended(phi, (("bx", 1), ("by", 2)), 1)
    padded = jnp.pad(padded, ((1, 1), (0, 0), (0, 0)))
    curv = curvature_of(padded)
    return slope * (first_residual[:, None, :] + second_residual[:, :, None]) - LAMBDA * curv


def solution(mesh):
    in_specs = (
        P("slab", "bx", "by"),
        P("slab", "by"),
        P("slab", "bx"),
        P("slab", "by"),
        P("slab", "bx"),
        P(),
    )
    out_specs = P("slab", "bx", "by")
    return jax.shard_map(
        per_device, mesh=mesh, in_specs=in_specs, out_specs=out_specs, check_vma=False
    )
```

profile of v0, /device:TPU:0, one launch (start us, length us, event | category | flops | bytes accessed | tf_op | source)
XLA Modules:
  0.0 121.4 jit_solution(6646163909018269001)
XLA Ops:
  6.5 0.0 all-reduce.3.cloned.1.call-start
  6.6 1.9 %fusion.10 = (f32[32,1,1024]{2,1,0:T(1,128)S(1)}, f32[32,1,1024]{2,1,0:T(1,128)S(1)}) fusion(f32[32,16,1024]{2,1,0:T(8,128)} %param.6), kind=kLoop, calls=%fused_computation.29 | loop fusion | bytes 524288 | tf_op jit(solution)/shard_map/slice | solution.py:15
  8.5 4.9 %collective-permute-start = (f32[32,1,1024]{2,0,1:T(8,128)S(1)}, f32[32,1,1024]{2,0,1:T(8,128)S(1)}, u32[]{:S(2)}, u32[]{:S(2)}) collective-permute-start(f32[32,1,1024]{2,0,1:T(8,128)S(1)} %copy.15), channel_id=1, source_target_pairs={{0,2},{2,4},{4,6},{6,8},{8,10},{10,12},{12,14},{1,3},{3,5},{5,7},{... | collective-permute-start | bytes 393224 | tf_op jit(solution)/shard_map/ppermute | solution.py:18
  13.5 1.3 %collective-permute-start.1 = (f32[32,1,1024]{2,0,1:T(8,128)S(1)}, f32[32,1,1024]{2,0,1:T(8,128)S(1)}, u32[]{:S(2)}, u32[]{:S(2)}) collective-permute-start(f32[32,1,1024]{2,0,1:T(8,128)S(1)} %copy.16), channel_id=1, source_target_pairs={{2,0},{4,2},{6,4},{8,6},{10,8},{12,10},{14,12},{3,1},{5,3},{7,5},{... | collective-permute-start | bytes 393224 | tf_op jit(solution)/shard_map/ppermute | solution.py:20
  14.8 2.9 %fusion.5 = (f32[32,1024]{1,0:T(8,128)}, f32[32,16]{1,0:T(8,128)S(1)}) fusion(f32[32,16,1024]{2,1,0:T(8,128)} %param.6), kind=kLoop, calls=%fused_computation.19 | loop fusion | flops 2063872 | bytes 2230272 | tf_op jit(solution)/shard_map/reduce_sum | solution.py:56
  17.7 0.0 all-reduce.3.cloned.1.call-update
  17.7 0.7 compare_select_fusion
  18.4 0.7 compare_and_fusion
  19.0 0.6 gather_fusion
  19.7 0.6 gather_fusion.1
  20.3 0.1 copy.9
  20.4 0.6 gather_fusion.2
  21.0 0.1 copy.10
  21.1 0.6 gather_fusion.3
  21.6 3.4 %psum.15 = f32[32,16]{1,0:T(8,128)S(1)} all-reduce(f32[32,16]{1,0:T(8,128)S(1)} %get-tuple-element.6), channel_id=1, replica_groups=mesh['slab'=2,'bx'=8,'by'=2] {'by'}, use_global_device_ids=true, to_apply=%region_3.4 | all-reduce | flops 512 | bytes 4096 | tf_op jit(solution)/shard_map/psum | solution.py:62
  25.0 0.1 subtract_multiply_fusion.1
  25.1 0.0 collective-permute-done
  25.1 0.1 copy.13
  25.2 0.1 copy.14
  25.4 0.5 pad_maximum_fusion
  25.9 1.7 %copy-done.3 = f32[32,18,1024]{2,1,0:T(8,128)} copy-done((f32[32,18,1024]{2,1,0:T(8,128)}, f32[32,18,1024]{2,1,0:T(8,128)S(1)}, u32[]{:S(2)}) %copy-start.3) | copy-done | bytes 2359320
  27.6 1.0 fusion.9
  28.6 2.3 %collective-permute-start.2 = (f32[32,18,1]{2,1,0:T(8,128)}, f32[32,18,1]{2,1,0:T(8,128)S(1)}, u32[]{:S(2)}, u32[]{:S(2)}) collective-permute-start(f32[32,18,1]{2,1,0:T(8,128)} %get-tuple-element.12), channel_id=1, source_target_pairs={{0,1},{2,3},{4,5},{6,7},{8,9},{10,11},{12,13},{14,15},{16,17},{18,... | collective-permute-start | bytes 6920 | tf_op jit(solution)/shard_map/ppermute | solution.py:18
  30.8 1.3 %collective-permute-start.3 = (f32[32,18,1]{2,1,0:T(8,128)}, f32[32,18,1]{2,1,0:T(8,128)}, u32[]{:S(2)}, u32[]{:S(2)}) collective-permute-start(f32[32,18,1]{2,1,0:T(8,128)} %get-tuple-element.11), channel_id=1, source_target_pairs={{1,0},{3,2},{5,4},{7,6},{9,8},{11,10},{13,12},{15,14},{17,16},{19,... | collective-permute-start | bytes 6920 | tf_op jit(solution)/shard_map/ppermute | solution.py:20
  32.1 58.6 %all-reduce.3.cloned.1.call-done = f32[32,1024]{1,0:T(8,128)} async-done(((f32[32,1024]{1,0:T(8,128)}), f32[32,1024]{1,0:T(8,128)}) %all-reduce.3.cloned.1.call-update) | async-done | bytes 131088 | tf_op jit(solution)/shard_map/psum | solution.py:64
  90.8 1.0 subtract_multiply_fusion
  91.8 0.0 collective-permute-done.2
  91.8 0.0 collective-permute-done.3
  91.8 4.8 %concatenate.7 = f32[32,18,1026]{2,1,0:T(8,128)} concatenate(f32[32,18,1]{2,1,0:T(8,128)S(1)} %collective-permute-done.2, f32[32,18,1024]{2,1,0:T(8,128)} %copy-done.3, f32[32,18,1]{2,1,0:T(8,128)} %collective-permute-done.3), dimensions={2} | concatenate | bytes 4727808 | tf_op jit(solution)/shard_map/concatenate | solution.py:16
  96.6 11.4 %fusion.6 = (f32[33,17,1025]{2,1,0:T(8,128)S(1)}, f32[33,17,1025]{2,1,0:T(8,128)S(1)}) fusion(f32[32,18,1026]{2,1,0:T(8,128)} %concatenate.7), kind=kLoop, calls=%fused_computation.20 | loop fusion | flops 6325275 | bytes 6964104 | tf_op jit(solution)/shard_map/div | solution.py:33
  108.1 1.5 %fusion.7 = (f32[33,17,1025]{2,1,0:T(8,128)S(1)}, f32[33,17,1025]{2,1,0:T(8,128)S(1)}) fusion(f32[33,17,1025]{2,1,0:T(8,128)S(1)} %get-tuple-element.8, f32[32,18,1026]{2,1,0:T(8,128)S(1)} %copy-done.1), kind=kLoop, calls=%fused_computation.21 | loop fusion | flops 2300100 | bytes 9264204 | tf_op jit(solution)/shard_map/div | solution.py:34
  109.6 4.9 %fusion.2 = f32[32,16,1024]{2,1,0:T(8,128)} fusion(f32[33,17,1025]{2,1,0:T(8,128)S(1)} %get-tuple-element.10, f32[33,17,1025]{2,1,0:T(8,128)S(1)} %get-tuple-element.9, f32[33,17,1025]{2,1,0:T(8,128)S(1)} %get-tuple-element.7, f32[32,16,1024]{2,1,0:T(8,128)S(1)} %copy-done.2, f32[32,16]{1,0:T(8,128)S(1)} %subtract_multiply_fusion.1, ...), kind=kLoop, calls=%fused_computation.13 | loop fusion | flops 6291456 | bytes 16910336 | tf_op jit(solution)/shard_map/sub | solution.py:69
  (17 shorter events, 0.1 us)
Async XLA Ops:
  6.5 12.5 %copy-start = (s32[64,1024]{1,0:T(8,128)S(1)}, s32[64,1024]{1,0:T(8,128)}, u32[]{:S(2)}) copy-start(s32[64,1024]{1,0:T(8,128)} %param.9) | copy-start | bytes 786436
  6.5 18.8 %copy-start.2 = (f32[32,16,1024]{2,1,0:T(8,128)S(1)}, f32[32,16,1024]{2,1,0:T(8,128)}, u32[]{:S(2)}) copy-start(f32[32,16,1024]{2,1,0:T(8,128)} %param.6) | copy-start | bytes 6291460
  6.5 13.1 %copy-start.4 = (f32[64,1024]{1,0:T(8,128)S(1)}, f32[64,1024]{1,0:T(8,128)}, u32[]{:S(2)}) copy-start(f32[64,1024]{1,0:T(8,128)} %param.7) | copy-start | bytes 786436
  6.5 13.8 %copy-start.5 = (s32[64,16]{0,1:T(8,128)S(1)}, s32[64,16]{0,1:T(8,128)}, u32[]{:S(2)}) copy-start(s32[64,16]{0,1:T(8,128)} %param.10) | copy-start | bytes 12292
  6.5 14.4 %copy-start.6 = (f32[64,16]{0,1:T(8,128)S(1)}, f32[64,16]{0,1:T(8,128)}, u32[]{:S(2)}) copy-start(f32[64,16]{0,1:T(8,128)} %param.8) | copy-start | bytes 12292
  6.5 84.2 %all-reduce.3.cloned.1.call-start = ((), (), s32[]{:S(2)}) async-start(), calls=%async_computation | async-start | bytes 262144 | tf_op jit(solution)/shard_map/psum | solution.py:64
  8.5 16.5 %collective-permute-start = (f32[32,1,1024]{2,0,1:T(8,128)S(1)}, f32[32,1,1024]{2,0,1:T(8,128)S(1)}, u32[]{:S(2)}, u32[]{:S(2)}) collective-permute-start(f32[32,1,1024]{2,0,1:T(8,128)S(1)} %copy.15), channel_id=1, source_target_pairs={{0,2},{2,4},{4,6},{6,8},{8,10},{10,12},{12,14},{1,3},{3,5},{5,7},{... | collective-permute-start | bytes 393224 | tf_op jit(solution)/shard_map/ppermute | solution.py:18
  13.5 11.7 %collective-permute-start.1 = (f32[32,1,1024]{2,0,1:T(8,128)S(1)}, f32[32,1,1024]{2,0,1:T(8,128)S(1)}, u32[]{:S(2)}, u32[]{:S(2)}) collective-permute-start(f32[32,1,1024]{2,0,1:T(8,128)S(1)} %copy.16), channel_id=1, source_target_pairs={{2,0},{4,2},{6,4},{8,6},{10,8},{12,10},{14,12},{3,1},{5,3},{7,5},{... | collective-permute-start | bytes 393224 | tf_op jit(solution)/shard_map/ppermute | solution.py:20
  25.9 1.7 %copy-start.3 = (f32[32,18,1024]{2,1,0:T(8,128)}, f32[32,18,1024]{2,1,0:T(8,128)S(1)}, u32[]{:S(2)}) copy-start(f32[32,18,1024]{2,1,0:T(8,128)S(1)} %pad_maximum_fusion) | copy-start | bytes 7077892
  28.6 63.2 %collective-permute-start.2 = (f32[32,18,1]{2,1,0:T(8,128)}, f32[32,18,1]{2,1,0:T(8,128)S(1)}, u32[]{:S(2)}, u32[]{:S(2)}) collective-permute-start(f32[32,18,1]{2,1,0:T(8,128)} %get-tuple-element.12), channel_id=1, source_target_pairs={{0,1},{2,3},{4,5},{6,7},{8,9},{10,11},{12,13},{14,15},{16,17},{18,... | collective-permute-start | bytes 6920 | tf_op jit(solution)/shard_map/ppermute | solution.py:18
  30.8 60.9 %collective-permute-start.3 = (f32[32,18,1]{2,1,0:T(8,128)}, f32[32,18,1]{2,1,0:T(8,128)}, u32[]{:S(2)}, u32[]{:S(2)}) collective-permute-start(f32[32,18,1]{2,1,0:T(8,128)} %get-tuple-element.11), channel_id=1, source_target_pairs={{1,0},{3,2},{5,4},{7,6},{9,8},{11,10},{13,12},{15,14},{17,16},{19,... | collective-permute-start | bytes 6920 | tf_op jit(solution)/shard_map/ppermute | solution.py:20
  96.6 11.4 %copy-start.1 = (f32[32,18,1026]{2,1,0:T(8,128)S(1)}, f32[32,18,1026]{2,1,0:T(8,128)}, u32[]{:S(2)}) copy-start(f32[32,18,1026]{2,1,0:T(8,128)} %concatenate.7) | copy-start | bytes 7091716
Sparse Core Ops, SparseCore 0:
  17.8 72.8 all-reduce.2
where the time goes:
time: 122 us; the launch traced here: 121 us
  waiting for transfers between devices  58.7 us (48%)
  other arithmetic  23.7 us (19%)
  between operations  13.6 us (11%)
  local copies, waits for them, and re-layouts  12.3 us (10%)
  starting transfers between devices  9.76 us (8%)
  blocking collectives  3.36 us (3%)
    psum x1, waiting for transfers between devices, per_device(): first_projection = lax.psum(part_a, 'bx') * (4.0 / total_x)  58.6 us
    div x1, other arithmetic, curvature_of(): flux_z = grad_z / magnitude  11.4 us
    ppermute x2, starting transfers between devices, extended(): lax.ppermute(tail, axis, [(i, (i + 1) % count) for i in range(ends)])  7.14 us
    sub x1, other arithmetic, per_device(): slope * (first_residual[:, None, :] + second_residual[:, :, None])  4.89 us
    concatenate x1, local copies, waits for them, and re-layouts, extended(): jnp.concatenate([lax.ppermute(tail, axis, [(i, (i + 1) % count) for i in...  4.83 us
    psum x1, blocking collectives, per_device(): second_projection = lax.psum(part_b, 'by') * (4.0 / total_y)  3.36 us
    reduce_sum x1, other arithmetic, per_device(): part_a = jnp.sum(heav, axis=1)  2.91 us
    ppermute x2, starting transfers between devices, extended(): lax.ppermute(head, axis, [((i + 1) % count, i) for i in range(ends)])  2.58 us
  transfers between devices with their start and end apart: 5, of which 1 were waited for; matrix products, arithmetic and copies ran while one was open for 8% of the time, Pallas kernels for 0%

commit v1 on v0

--- a/solution.py
+++ b/solution.py
@@ -61,7 +61,7 @@
     second_mask_rows = jnp.take(second_view_mask, plane_detector_rows, axis=0).astype(jnp.float32)
     second_projection = lax.psum(part_b, "by") * (4.0 / total_y)
     second_residual = second_mask_rows * (second_projection - second_measured_rows)
-    first_projection = lax.psum(part_a, "bx") * (4.0 / total_x)
+    first_projection = jnp.sum(lax.all_gather(part_a, "bx"), axis=0) * (4.0 / total_x)
     first_residual = first_mask_rows * (first_projection - first_measured_rows)
     padded = extended(phi, (("bx", 1), ("by", 2)), 1)
     padded = jnp.pad(padded, ((1, 1), (0, 0), (0, 0)))

time: 122 us -> 79 us (0.65)
  waiting for transfers between devices: 58.7 us -> 6.31 us
  other arithmetic: 23.7 us -> 31.9 us
  local copies, waits for them, and re-layouts: 12.3 us -> 13.7 us
    psum x1 -> x0, waiting for transfers between devices: 58.6 us -> none  [per_device(): first_projection = lax.psum(part_a, 'bx') * (4.0 / total_x)]
    all_gather x0 -> x1, waiting for transfers between devices: none -> 4.96 us  [per_device(): lax.all_gather(part_a, 'bx')]
    sub x1, other arithmetic: 4.89 us -> 9.85 us  [per_device(): slope * (first_residual[:, None, :] + second_residual[:, :, None])]
    div x1, other arithmetic: 1.54 us -> 3.78 us  [curvature_of(): flux_x = grad_x / magnitude]
    unnamed x18 -> x16, local copies, waits for them, and re-layouts: 1.92 us -> 3.26 us
    ppermute x2, waiting for transfers between devices: 0.01 us -> 1.32 us  [extended(): lax.ppermute(head, axis, [((i + 1) % count, i) for i in range(ends)])]
    reduce_sum x0 -> x1, other arithmetic: none -> 1.29 us  [per_device(): jnp.sum(lax.all_gather(part_a, 'bx'), axis=0) * (4.0 / total_x)]
    div x1, other arithmetic: 11.4 us -> 12.7 us  [curvature_of(): flux_z = grad_z / magnitude]
  transfers between devices with their start and end apart: 5 -> 5, of which waited for: 1 -> 2; matrix products, arithmetic and copies ran while one was open for 8% -> 39% of each run, Pallas kernels for 0% -> 0%
where the time goes in v1:
time: 79 us; the launch traced here: 78.6 us
  other arithmetic  31.9 us (40%)
  local copies, waits for them, and re-layouts  13.7 us (17%)
  between operations  13.6 us (17%)
  starting transfers between devices  9.72 us (12%)
  waiting for transfers between devices  6.31 us (8%)
  blocking collectives  3.36 us (4%)
    div x1, other arithmetic, curvature_of(): flux_z = grad_z / magnitude  12.7 us
    sub x1, other arithmetic, per_device(): slope * (first_residual[:, None, :] + second_residual[:, :, None])  9.85 us
    ppermute x2, starting transfers between devices, extended(): lax.ppermute(tail, axis, [(i, (i + 1) % count) for i in range(ends)])  7.13 us
    all_gather x1, waiting for transfers between devices, per_device(): lax.all_gather(part_a, 'bx')  4.96 us
    concatenate x1, local copies, waits for them, and re-layouts, extended(): jnp.concatenate([lax.ppermute(tail, axis, [(i, (i + 1) % count) for i in...  4.89 us
    div x1, other arithmetic, curvature_of(): flux_x = grad_x / magnitude  3.78 us
    psum x1, blocking collectives, per_device(): second_projection = lax.psum(part_b, 'by') * (4.0 / total_y)  3.36 us
    unnamed x16, local copies, waits for them, and re-layouts  3.26 us
  transfers between devices with their start and end apart: 5, of which 2 were waited for; matrix products, arithmetic and copies ran while one was open for 39% of the time, Pallas kernels for 0%

profile of v1, /device:TPU:0, one launch (start us, length us, event | category | flops | bytes accessed | tf_op | source)
XLA Modules:
  0.0 78.6 jit_solution(5808721985318435154)
XLA Ops:
  6.5 1.9 %fusion.10 = (f32[32,1,1024]{2,1,0:T(1,128)S(1)}, f32[32,1,1024]{2,1,0:T(1,128)S(1)}) fusion(f32[32,16,1024]{2,1,0:T(8,128)} %param.6), kind=kLoop, calls=%fused_computation.29 | loop fusion | bytes 524288 | tf_op jit(solution)/shard_map/slice | solution.py:15
  8.5 4.9 %collective-permute-start = (f32[32,1,1024]{2,0,1:T(8,128)S(1)}, f32[32,1,1024]{2,0,1:T(8,128)S(1)}, u32[]{:S(2)}, u32[]{:S(2)}) collective-permute-start(f32[32,1,1024]{2,0,1:T(8,128)S(1)} %copy.21), channel_id=1, source_target_pairs={{0,2},{2,4},{4,6},{6,8},{8,10},{10,12},{12,14},{1,3},{3,5},{5,7},{... | collective-permute-start | bytes 393224 | tf_op jit(solution)/shard_map/ppermute | solution.py:18
  13.4 1.3 %collective-permute-start.1 = (f32[32,1,1024]{2,0,1:T(8,128)S(1)}, f32[32,1,1024]{2,0,1:T(8,128)S(1)}, u32[]{:S(2)}, u32[]{:S(2)}) collective-permute-start(f32[32,1,1024]{2,0,1:T(8,128)S(1)} %copy.22), channel_id=1, source_target_pairs={{2,0},{4,2},{6,4},{8,6},{10,8},{12,10},{14,12},{3,1},{5,3},{7,5},{... | collective-permute-start | bytes 393224 | tf_op jit(solution)/shard_map/ppermute | solution.py:20
  14.7 2.9 %fusion.5 = (f32[32,1024]{1,0:T(8,128)}, f32[32,16]{1,0:T(8,128)S(1)}) fusion(f32[32,16,1024]{2,1,0:T(8,128)} %param.6), kind=kLoop, calls=%fused_computation.19 | loop fusion | flops 2063872 | bytes 2230272 | tf_op jit(solution)/shard_map/reduce_sum | solution.py:56
  17.6 0.0 all-gather.3.cloned.1.call-update
  17.7 0.7 compare_select_fusion
  18.3 0.8 copy.15
  19.1 0.8 copy.16
  19.9 0.6 gather_fusion.2
  20.5 0.6 gather_fusion.3
  21.0 3.4 %psum.7 = f32[32,16]{1,0:T(8,128)S(1)} all-reduce(f32[32,16]{1,0:T(8,128)S(1)} %get-tuple-element.6), channel_id=1, replica_groups=mesh['slab'=2,'bx'=8,'by'=2] {'by'}, use_global_device_ids=true, to_apply=%region_3.4 | all-reduce | flops 512 | bytes 4096 | tf_op jit(solution)/shard_map/psum | solution.py:62
  24.4 0.0 collective-permute-done
  24.4 0.1 copy.19
  24.6 0.1 copy.20
  24.7 0.0 copy-start.4
  24.8 0.5 pad_maximum_fusion
  25.3 1.6 %copy-done.3 = f32[32,18,1024]{2,1,0:T(8,128)} copy-done((f32[32,18,1024]{2,1,0:T(8,128)}, f32[32,18,1024]{2,1,0:T(8,128)S(1)}, u32[]{:S(2)}) %copy-start.3) | copy-done | bytes 2359320
  26.9 1.0 %fusion.9 = (f32[32,18,1]{2,1,0:T(8,128)}, f32[32,18,1]{2,1,0:T(8,128)}) fusion(f32[32,18,1024]{2,1,0:T(8,128)S(1)} %pad_maximum_fusion), kind=kLoop, calls=%fused_computation.28 | loop fusion | bytes 9216 | tf_op jit(solution)/shard_map/slice | solution.py:14
  28.0 2.3 %collective-permute-start.2 = (f32[32,18,1]{2,1,0:T(8,128)}, f32[32,18,1]{2,1,0:T(8,128)S(1)}, u32[]{:S(2)}, u32[]{:S(2)}) collective-permute-start(f32[32,18,1]{2,1,0:T(8,128)} %get-tuple-element.12), channel_id=1, source_target_pairs={{0,1},{2,3},{4,5},{6,7},{8,9},{10,11},{12,13},{14,15},{16,17},{18,... | collective-permute-start | bytes 6920 | tf_op jit(solution)/shard_map/ppermute | solution.py:18
  30.2 1.3 %collective-permute-start.3 = (f32[32,18,1]{2,1,0:T(8,128)}, f32[32,18,1]{2,1,0:T(8,128)}, u32[]{:S(2)}, u32[]{:S(2)}) collective-permute-start(f32[32,18,1]{2,1,0:T(8,128)} %get-tuple-element.11), channel_id=1, source_target_pairs={{1,0},{3,2},{5,4},{7,6},{9,8},{11,10},{13,12},{15,14},{17,16},{19,... | collective-permute-start | bytes 6920 | tf_op jit(solution)/shard_map/ppermute | solution.py:20
  31.5 0.1 subtract_multiply_fusion.1
  31.6 0.6 gather_fusion
  32.2 0.6 gather_fusion.1
  32.8 0.0 collective-permute-done.2
  32.9 1.3 %collective-permute-done.3 = f32[32,18,1]{2,1,0:T(8,128)} collective-permute-done((f32[32,18,1]{2,1,0:T(8,128)}, f32[32,18,1]{2,1,0:T(8,128)}, u32[]{:S(2)}, u32[]{:S(2)}) %collective-permute-start.3) | collective-permute-done | bytes 2336 | tf_op jit(solution)/shard_map/ppermute | solution.py:20
  34.2 4.9 %concatenate.7 = f32[32,18,1026]{2,1,0:T(8,128)} concatenate(f32[32,18,1]{2,1,0:T(8,128)S(1)} %collective-permute-done.2, f32[32,18,1024]{2,1,0:T(8,128)} %copy-done.3, f32[32,18,1]{2,1,0:T(8,128)} %collective-permute-done.3), dimensions={2} | concatenate | bytes 4727808 | tf_op jit(solution)/shard_map/concatenate | solution.py:16
  39.1 12.7 %fusion.6 = (f32[33,17,1025]{2,1,0:T(8,128)}, f32[33,17,1025]{2,1,0:T(8,128)S(1)}) fusion(f32[32,18,1026]{2,1,0:T(8,128)} %concatenate.7), kind=kLoop, calls=%fused_computation.20 | loop fusion | flops 6325275 | bytes 6964104 | tf_op jit(solution)/shard_map/div | solution.py:33
  51.8 3.8 %fusion.7 = (f32[33,17,1025]{2,1,0:T(8,128)}, f32[33,17,1025]{2,1,0:T(8,128)}) fusion(f32[33,17,1025]{2,1,0:T(8,128)S(1)} %get-tuple-element.8, f32[32,18,1026]{2,1,0:T(8,128)S(1)} %copy-done.1), kind=kLoop, calls=%fused_computation.21 | loop fusion | flops 2300100 | bytes 9264204 | tf_op jit(solution)/shard_map/div | solution.py:34
  55.5 5.0 %all-gather.3.cloned.1.call-done = f32[256,1024]{1,0:T(8,128)} async-done(((f32[32,1024]{1,0:T(8,128)}), f32[256,1024]{1,0:T(8,128)}) %all-gather.3.cloned.1.call-update) | async-done | bytes 1048592 | tf_op jit(solution)/shard_map/all_gather | solution.py:64
  60.5 1.3 %reduce_sum.28 = f32[32,1024]{1,0:T(8,128)S(1)} reduce(f32[8,32,1024]{2,1,0:T(8,128)} %bitcast.1, f32[]{:T(128)} %constant.62.clone.1), dimensions={0}, to_apply=%region_1.0 | reduce | flops 229376 | bytes 1179652 | tf_op jit(solution)/shard_map/reduce_sum | solution.py:64
  61.8 0.1 subtract_multiply_fusion
  61.9 9.8 %fusion.2 = f32[32,16,1024]{2,1,0:T(8,128)} fusion(f32[33,17,1025]{2,1,0:T(8,128)} %get-tuple-element.10, f32[33,17,1025]{2,1,0:T(8,128)} %get-tuple-element.9, f32[33,17,1025]{2,1,0:T(8,128)} %get-tuple-element.7, f32[32,16,1024]{2,1,0:T(8,128)S(1)} %copy-done.2, f32[32,16]{1,0:T(8,128)S(1)} %subtract_multiply_fusion.1, f32[32,1024]{1,0:T(8,128)S(1)} %subtract_multiply_fusion), kind=kLoop, calls=%fused_computation.13 | loop fusion | flops 6291456 | bytes 16910336 | tf_op jit(solution)/shard_map/sub | solution.py:69
  (16 shorter events, 0.1 us)
Async XLA Ops:
  6.5 25.1 %copy-start = (s32[64,1024]{1,0:T(8,128)S(1)}, s32[64,1024]{1,0:T(8,128)}, u32[]{:S(2)}) copy-start(s32[64,1024]{1,0:T(8,128)} %param.9) | copy-start | bytes 786436
  6.5 18.2 %copy-start.2 = (f32[32,16,1024]{2,1,0:T(8,128)S(1)}, f32[32,16,1024]{2,1,0:T(8,128)}, u32[]{:S(2)}) copy-start(f32[32,16,1024]{2,1,0:T(8,128)} %param.6) | copy-start | bytes 6291460
  6.5 17.9 %copy-start.5 = (s32[32]{0:T(128)S(1)}, s32[32]{0:T(128)}, u32[]{:S(2)}) copy-start(s32[32]{0:T(128)} %param.11) | copy-start | bytes 388
  6.5 54.0 %all-gather.3.cloned.1.call-start = ((), (), s32[]{:S(2)}) async-start(), calls=%async_computation | async-start | bytes 1179648 | tf_op jit(solution)/shard_map/all_gather | solution.py:64
  8.5 15.9 %collective-permute-start = (f32[32,1,1024]{2,0,1:T(8,128)S(1)}, f32[32,1,1024]{2,0,1:T(8,128)S(1)}, u32[]{:S(2)}, u32[]{:S(2)}) collective-permute-start(f32[32,1,1024]{2,0,1:T(8,128)S(1)} %copy.21), channel_id=1, source_target_pairs={{0,2},{2,4},{4,6},{6,8},{8,10},{10,12},{12,14},{1,3},{3,5},{5,7},{... | collective-permute-start | bytes 393224 | tf_op jit(solution)/shard_map/ppermute | solution.py:18
  13.4 11.2 %collective-permute-start.1 = (f32[32,1,1024]{2,0,1:T(8,128)S(1)}, f32[32,1,1024]{2,0,1:T(8,128)S(1)}, u32[]{:S(2)}, u32[]{:S(2)}) collective-permute-start(f32[32,1,1024]{2,0,1:T(8,128)S(1)} %copy.22), channel_id=1, source_target_pairs={{2,0},{4,2},{6,4},{8,6},{10,8},{12,10},{14,12},{3,1},{5,3},{7,5},{... | collective-permute-start | bytes 393224 | tf_op jit(solution)/shard_map/ppermute | solution.py:20
  24.7 7.5 %copy-start.4 = (f32[64,1024]{1,0:T(8,128)S(1)}, f32[64,1024]{1,0:T(8,128)}, u32[]{:S(2)}) copy-start(f32[64,1024]{1,0:T(8,128)} %param.7) | copy-start | bytes 786436
  25.3 1.6 %copy-start.3 = (f32[32,18,1024]{2,1,0:T(8,128)}, f32[32,18,1024]{2,1,0:T(8,128)S(1)}, u32[]{:S(2)}) copy-start(f32[32,18,1024]{2,1,0:T(8,128)S(1)} %pad_maximum_fusion) | copy-start | bytes 7077892
  28.0 4.9 %collective-permute-start.2 = (f32[32,18,1]{2,1,0:T(8,128)}, f32[32,18,1]{2,1,0:T(8,128)S(1)}, u32[]{:S(2)}, u32[]{:S(2)}) collective-permute-start(f32[32,18,1]{2,1,0:T(8,128)} %get-tuple-element.12), channel_id=1, source_target_pairs={{0,1},{2,3},{4,5},{6,7},{8,9},{10,11},{12,13},{14,15},{16,17},{18,... | collective-permute-start | bytes 6920 | tf_op jit(solution)/shard_map/ppermute | solution.py:18
  30.2 4.0 %collective-permute-start.3 = (f32[32,18,1]{2,1,0:T(8,128)}, f32[32,18,1]{2,1,0:T(8,128)}, u32[]{:S(2)}, u32[]{:S(2)}) collective-permute-start(f32[32,18,1]{2,1,0:T(8,128)} %get-tuple-element.11), channel_id=1, source_target_pairs={{1,0},{3,2},{5,4},{7,6},{9,8},{11,10},{13,12},{15,14},{17,16},{19,... | collective-permute-start | bytes 6920 | tf_op jit(solution)/shard_map/ppermute | solution.py:20
  39.1 12.7 %copy-start.1 = (f32[32,18,1026]{2,1,0:T(8,128)S(1)}, f32[32,18,1026]{2,1,0:T(8,128)}, u32[]{:S(2)}) copy-start(f32[32,18,1026]{2,1,0:T(8,128)} %concatenate.7) | copy-start | bytes 7091716
Sparse Core Ops, SparseCore 0:
  17.8 42.6 all-gather.2
